TPU v7x, 512 devices: a whole 4x8x8 slice. The times are simulated.
512 devices in a mesh: shell: 8 (over z), row: 4 (over x_hi, core), col: 16 (over x_lo, y).
Axes of the slice: x: 4 (x_hi: 2, x_lo: 2; x = x_hi * 2 + x_lo), y: 8, z: 8, core: 2. Of those that a mesh axis runs over, the one named last changes fastest.
Arguments:
- left_basis: bfloat16 [2, 4096, 6144], P(None, 'row', 'shell'), may hold values from -6 to 6
- right_basis: bfloat16 [2, 6144, 8192], P(None, 'shell', 'col'), may hold values from -0.078125 to 0.078125
- point_weight: float32 [6144], P('shell'), may hold values from 0.3 to 3
- shell_index: int32 [6144], P('shell'), may hold values from 0 to 11
- green_table: float32 [12, 2], replicated, may hold values from -4 to 4
- pivot_rows: int32 [512], replicated, may hold values from 0 to 4095, as said below
- diag_inverse: bfloat16 [2, 512, 512], replicated, may hold values from -0.005859375 to 0.005859375
Outputs:
- factored: float32 [2, 4, 8, 128, 8192], P(None, 'row', 'shell', None, 'col')
Inputs may be any that keep to these rules, and one draw needn't show every extreme that they name: `pivot_rows`: 512 distinct matrix rows.
All inputs are finite; a program needn't handle non-finite values.
Results may differ from a plain program's by a relative error of at most 0.0056.
Values may be sent and summed in bfloat16 or wider, within the bound.
No kernel may reach another device: no remote copies, remote signals or barrier semaphores. Data moves between devices by JAX's collectives and lax.ppermute only.
A program may use at most 128 MiB of HBM per device.

v0:
```python
import jax
import jax.numpy as jnp
from jax import lax
from jax.sharding import PartitionSpec as P


def broadcast(block, axis, source):
    block = jnp.where(lax.axis_index(axis) == source, block, jnp.zeros_like(block))
    return lax.psum(block, axis)


def complex_block(real_part, imag_part):
    upper_half = jnp.concatenate([real_part, imag_part], axis=1)
    lower_half = jnp.concatenate([-imag_part, real_part], axis=1)
    return jnp.concatenate([upper_half, lower_half], axis=0)


def weigh_points(right_basis, point_weight, shell_index, green_table):
    shells_count = green_table.shape[0]
    matches = shell_index[:, None] == jnp.arange(shells_count, dtype=jnp.int32)[None, :]
    green_real = jnp.sum(jnp.where(matches, green_table[None, :, 0], 0.0), axis=1)
    green_imag = jnp.sum(jnp.where(matches, green_table[None, :, 1], 0.0), axis=1)
    weight_real = point_weight * green_real
    weight_imag = point_weight * green_imag
    basis_real = right_basis[0].astype(jnp.float32)
    basis_imag = right_basis[1].astype(jnp.float32)
    weighted_real = (weight_real[:, None] * basis_real - weight_imag[:, None] * basis_imag).astype(
        jnp.bfloat16
    )
    weighted_imag = (weight_real[:, None] * basis_imag + weight_imag[:, None] * basis_real).astype(
        jnp.bfloat16
    )
    return (weighted_real, weighted_imag)


def reduce_tiles(term_rows, owned_rows):
    return lax.psum_scatter(
        term_rows(jnp.int32(0), owned_rows * lax.axis_size("shell")),
        "shell",
        scatter_dimension=0,
        tiled=True,
    )


def pick_rows(matrix_rows, pivot_rows, row_base):
    held_rows = matrix_rows.shape[0]
    local_index = pivot_rows - row_base
    inside = (local_index >= 0) & (local_index < held_rows)
    picked = jnp.take(matrix_rows, jnp.clip(local_index, 0, held_rows - 1), axis=0)
    return jnp.where(inside[:, None], picked, 0.0)


def select_pivots(coupling, pivot_rows, row_base):
    picked = pick_rows(coupling, pivot_rows, row_base).astype(jnp.bfloat16)
    return lax.psum(picked, ("shell", "row")).astype(jnp.float32).astype(jnp.bfloat16)


def body(left_basis, right_basis, point_weight, shell_index, green_table, pivot_rows, diag_inverse):
    shells = lax.axis_size("shell")
    owned_rows = left_basis.shape[1] // shells
    panel_width = right_basis.shape[2]
    weighted_real, weighted_imag = weigh_points(right_basis, point_weight, shell_index, green_table)
    grid_row = lax.axis_index("row")
    shell_rank = lax.axis_index("shell")
    row_base = (grid_row * shells + shell_rank) * owned_rows
    left_stack = jnp.concatenate([left_basis[0], left_basis[1]], axis=1)
    right_stack = complex_block(weighted_real, weighted_imag)

    def from_bases(first_row, row_count):
        return jnp.dot(left_stack, right_stack, preferred_element_type=jnp.float32)

    coupling = reduce_tiles(from_bases, owned_rows)
    pivot_sum = select_pivots(coupling, pivot_rows, row_base)
    panel_real = coupling[:, :panel_width]
    panel_imag = coupling[:, panel_width:]
    inverse_real = diag_inverse[0].astype(jnp.float32)
    inverse_imag = diag_inverse[1].astype(jnp.float32)
    highest = lax.Precision.HIGHEST
    mult_real = (
        jnp.dot(panel_real, inverse_real, precision=highest, preferred_element_type=jnp.float32)
        - jnp.dot(panel_imag, inverse_imag, precision=highest, preferred_element_type=jnp.float32)
    ).astype(jnp.bfloat16)
    mult_imag = (
        jnp.dot(panel_real, inverse_imag, precision=highest, preferred_element_type=jnp.float32)
        + jnp.dot(panel_imag, inverse_real, precision=highest, preferred_element_type=jnp.float32)
    ).astype(jnp.bfloat16)
    multipliers = jnp.concatenate([mult_real, mult_imag], axis=1)
    multipliers = broadcast(multipliers, "col", 0)
    pivot_block = complex_block(pivot_sum[:, :panel_width], pivot_sum[:, panel_width:])
    update = jnp.dot(multipliers, pivot_block, preferred_element_type=jnp.float32)
    updated = coupling - update
    return jnp.stack([updated[:, :panel_width], updated[:, panel_width:]]).reshape(
        2, 1, 1, owned_rows, panel_width
    )


def solution(mesh):
    return jax.shard_map(
        body,
        mesh=mesh,
        in_specs=(
            P(None, "row", "shell"),
            P(None, "shell", "col"),
            P("shell"),
            P("shell"),
            P(),
            P(),
            P(),
        ),
        out_specs=P(None, "row", "shell", None, "col"),
        check_vma=False,
    )
```

profile of v0, /device:TPU:4, one launch (start us, length us, event | category | flops | bytes accessed | tf_op | source)
XLA Modules:
  0.0 509.2 jit_solution(4400206457405959289)
XLA Ops:
  6.5 0.8 slice_bitcast_fusion.4
  7.4 0.8 select_reduce_fusion.1
  8.1 0.7 fusion.44
  8.8 1.9 fusion.42
  10.8 0.4 fusion.18
  11.2 0.2 slice_bitcast_fusion.1
  11.4 5.3 %fusion = f32[1024,1024]{1,0:T(8,128)} fusion(bf16[1024,768]{1,0:T(8,128)(2,1)S(1)} %get-tuple-element.12, bf16[1024,768]{1,0:T(8,128)(2,1)S(1)} %get-tuple-element.11, bf16[768,512]{1,0:T(8,128)(2,1)S(1)} %fusion.18, bf16[768,512]{1,0:T(8,128)(2,1)S(1)} %get-tuple-element.9, bf16[768,512]{1,0:T(8,128)(2,1)S(1)} %get-tuple-element.10), kind=kOutput, calls=%fused_computation.1 | convolution fusion | flops 3240099840 | bytes 9699328 | tf_op jit(solution)/shard_map/dot_general | solution.py:70
  16.8 0.0 all-reduce.5.cloned.1.call-start
  16.8 0.6 copy-done.5
  17.4 62.8 %reduce-scatter.2.cloned.1.call-done = f32[128,1024]{1,0:T(8,128)} async-done(((f32[1024,1024]{1,0:T(8,128)}), f32[128,1024]{1,0:T(8,128)}) %reduce-scatter.2.cloned.1.call-update) | async-done | bytes 524304 | tf_op jit(solution)/shard_map/reduce_scatter | solution.py:37
  80.3 3.8 gather_fusion
  84.1 1.4 select_convert_fusion
  85.4 0.0 all-reduce.3.cloned.1.call-start
  85.5 0.2 copy-done.2
  85.7 0.4 fusion.30
  86.1 0.4 fusion.26
  86.4 0.4 fusion.24
  86.8 0.4 fusion.25
  87.2 0.8 maximum_select_fusion
  88.0 267.2 %all-reduce.5.cloned.1.call-done = bf16[512,1024]{1,0:T(8,128)(2,1)} async-done(((bf16[512,1024]{1,0:T(8,128)(2,1)}), bf16[512,1024]{1,0:T(8,128)(2,1)}) %all-reduce.5.cloned.1.call-update) | async-done | bytes 1048592 | tf_op jit(solution)/shard_map/psum | solution.py:55
  355.2 1.4 slice_negate_fusion
  356.6 143.8 %all-reduce.3.cloned.1.call-done = bf16[128,1024]{1,0:T(8,128)(2,1)} async-done(((bf16[128,1024]{1,0:T(8,128)(2,1)}), bf16[128,1024]{1,0:T(8,128)(2,1)}) %all-reduce.3.cloned.1.call-update) | async-done | bytes 262160 | tf_op jit(solution)/shard_map/psum | solution.py:9
  500.4 1.4 fusion.21
  501.8 0.8 maximum_bitcast_fusion
  (17 shorter events, 0.1 us)
Async XLA Ops:
  6.5 4.2 copy-start.1
  6.5 73.7 %reduce-scatter.2.cloned.1.call-start = ((), (), s32[]{:S(2)}) async-start(), calls=%async_computation.1 | async-start | bytes 4718592 | tf_op jit(solution)/shard_map/reduce_scatter | solution.py:37
  8.8 2.4 copy-start.3
  16.7 0.7 copy-start.5
  16.8 338.4 %all-reduce.5.cloned.1.call-start = ((), (), s32[]{:S(2)}) async-start(), calls=%async_computation.3 | async-start | bytes 2097152 | tf_op jit(solution)/shard_map/psum | solution.py:55
  84.0 1.5 copy-start
  84.0 1.6 copy-start.2
  85.4 414.9 %all-reduce.3.cloned.1.call-start = ((), (), s32[]{:S(2)}) async-start(), calls=%async_computation.2 | async-start | bytes 524288 | tf_op jit(solution)/shard_map/psum | solution.py:9
  355.2 145.2 %copy-start.4 = (bf16[512,1024]{1,0:T(8,128)(2,1)S(1)}, bf16[512,1024]{1,0:T(8,128)(2,1)}, u32[]{:S(2)}) copy-start(bf16[512,1024]{1,0:T(8,128)(2,1)} %all-reduce.5.cloned.1.call-done) | copy-start | bytes 3145732
Sparse Core Ops, SparseCore 0:
  16.9 63.3 reduce-scatter.1
  85.6 269.6 all-reduce.4
  358.4 141.9 all-reduce.2
where the time goes:
time: 509 us
  waiting for transfers between devices  474 us (93%)
  between operations  13.2 us (3%)
  matrix products  8.23 us (2%)
  other arithmetic  8.1 us (2%)
  local copies, waits for them, and re-layouts  5.65 us (1%)
    psum x1, waiting for transfers between devices, select_pivots(): lax.psum(picked, ('shell', 'row')).astype(jnp.float32).astype(jnp.bfloat16)  267 us
    psum x1, waiting for transfers between devices, broadcast(): return lax.psum(block, axis)  144 us
    reduce_scatter x1, waiting for transfers between devices, reduce_tiles(): lax.psum_scatter(term_rows(jnp.int32(0), owned_rows * lax.axis_size('shel...  62.8 us
  transfers between devices with their start and end apart: 3, of which 3 were waited for; matrix products, arithmetic and copies ran while one was open for 1% of the time, Pallas kernels for 0%

commit v1 on v0

--- a/solution.py
+++ b/solution.py
@@ -52,7 +52,7 @@
 
 def select_pivots(coupling, pivot_rows, row_base):
     picked = pick_rows(coupling, pivot_rows, row_base).astype(jnp.bfloat16)
-    return lax.psum(picked, ("shell", "row")).astype(jnp.float32).astype(jnp.bfloat16)
+    return lax.psum(lax.psum(picked, "row"), "shell").astype(jnp.float32).astype(jnp.bfloat16)
 
 
 def body(left_basis, right_basis, point_weight, shell_index, green_table, pivot_rows, diag_inverse):

time: 509 us -> 373 us (0.73)
  waiting for transfers between devices: 474 us -> 338 us
    psum x1 -> x2, waiting for transfers between devices: 267 us -> 136 us  [the longest x1 84 us: select_pivots(): lax.psum(lax.psum(picked, 'row'), 'shell').astype(jnp.float32)]
    psum x1, waiting for transfers between devices: 144 us -> 139 us  [broadcast(): return lax.psum(block, axis)]
  transfers between devices with their start and end apart: 3 -> 4, of which waited for: 3 -> 4; matrix products, arithmetic and copies ran while one was open for 1% -> 1% of each run, Pallas kernels for 0% -> 0%
where the time goes in v1:
time: 373 us
  waiting for transfers between devices  338 us (91%)
  between operations  13.3 us (4%)
  matrix products  8.23 us (2%)
  other arithmetic  8.1 us (2%)
  local copies, waits for them, and re-layouts  5.46 us (1%)
    psum x1, waiting for transfers between devices, broadcast(): return lax.psum(block, axis)  139 us
    psum x1, waiting for transfers between devices, select_pivots(): lax.psum(lax.psum(picked, 'row'), 'shell').astype(jnp.float32)  84 us
    reduce_scatter x1, waiting for transfers between devices, reduce_tiles(): lax.psum_scatter(term_rows(jnp.int32(0), owned_rows * lax.axis_size('shel...  62.8 us
    psum x1, waiting for transfers between devices, select_pivots(): lax.psum(picked, 'row')  52.3 us
  transfers between devices with their start and end apart: 4, of which 4 were waited for; matrix products, arithmetic and copies ran while one was open for 1% of the time, Pallas kernels for 0%

profile of v1, /device:TPU:4, one launch (start us, length us, event | category | flops | bytes accessed | tf_op | source)
XLA Modules:
  0.0 373.0 jit_solution(9975835405656101490)
XLA Ops:
  6.5 0.8 slice_bitcast_fusion.4
  7.4 0.8 select_reduce_fusion.1
  8.1 0.7 fusion.44
  8.8 1.9 fusion.42
  10.8 0.4 fusion.18
  11.2 0.2 slice_bitcast_fusion.1
  11.4 5.3 %fusion = f32[1024,1024]{1,0:T(8,128)} fusion(bf16[1024,768]{1,0:T(8,128)(2,1)S(1)} %get-tuple-element.12, bf16[1024,768]{1,0:T(8,128)(2,1)S(1)} %get-tuple-element.11, bf16[768,512]{1,0:T(8,128)(2,1)S(1)} %fusion.18, bf16[768,512]{1,0:T(8,128)(2,1)S(1)} %get-tuple-element.9, bf16[768,512]{1,0:T(8,128)(2,1)S(1)} %get-tuple-element.10), kind=kOutput, calls=%fused_computation.1 | convolution fusion | flops 3240099840 | bytes 9699328 | tf_op jit(solution)/shard_map/dot_general | solution.py:70
  16.8 0.0 all-reduce.6.cloned.1.call-start
  16.8 0.6 copy-done.5
  17.4 62.8 %reduce-scatter.2.cloned.1.call-done = f32[128,1024]{1,0:T(8,128)} async-done(((f32[1024,1024]{1,0:T(8,128)}), f32[128,1024]{1,0:T(8,128)}) %reduce-scatter.2.cloned.1.call-update) | async-done | bytes 524304 | tf_op jit(solution)/shard_map/reduce_scatter | solution.py:37
  80.3 3.8 %gather_fusion = bf16[512,1024]{1,0:T(8,128)(2,1)S(1)} fusion(f32[128,1024]{1,0:T(8,128)} %reduce-scatter.2.cloned.1.call-done, s32[1024]{0:T(1024)S(1)} %pad_clamp_fusion), kind=kCustom, calls=%fused_computation | custom fusion | bytes 2099200 | tf_op jit(solution)/shard_map/jit(_take)/gather | solution.py:49
  84.1 1.4 select_convert_fusion
  85.4 0.0 all-reduce.8.cloned.1.call-start
  85.5 52.3 %all-reduce.6.cloned.1.call-done = bf16[512,1024]{1,0:T(8,128)(2,1)} async-done(((bf16[512,1024]{1,0:T(8,128)(2,1)}), bf16[512,1024]{1,0:T(8,128)(2,1)}) %all-reduce.6.cloned.1.call-update) | async-done | bytes 1048592 | tf_op jit(solution)/shard_map/psum | solution.py:55
  137.9 0.4 fusion.30
  138.3 0.4 fusion.26
  138.6 0.4 fusion.24
  139.0 0.4 fusion.25
  139.4 0.8 maximum_select_fusion
  140.2 84.0 %all-reduce.8.cloned.1.call-done = bf16[512,1024]{1,0:T(8,128)(2,1)} async-done(((bf16[512,1024]{1,0:T(8,128)(2,1)}), bf16[512,1024]{1,0:T(8,128)(2,1)}) %all-reduce.8.cloned.1.call-update) | async-done | bytes 1048592 | tf_op jit(solution)/shard_map/psum | solution.py:55
  224.2 1.4 slice_negate_fusion
  225.5 138.6 %all-reduce.4.cloned.1.call-done = bf16[128,1024]{1,0:T(8,128)(2,1)} async-done(((bf16[128,1024]{1,0:T(8,128)(2,1)}), bf16[128,1024]{1,0:T(8,128)(2,1)}) %all-reduce.4.cloned.1.call-update) | async-done | bytes 262160 | tf_op jit(solution)/shard_map/psum | solution.py:9
  364.1 1.4 fusion.21
  365.6 0.8 maximum_bitcast_fusion
  (20 shorter events, 0.2 us)
Async XLA Ops:
  6.5 4.2 %copy-start.1 = (bf16[2,768,512]{2,1,0:T(8,128)(2,1)S(1)}, bf16[2,768,512]{2,1,0:T(8,128)(2,1)}, u32[]{:S(2)}) copy-start(bf16[2,768,512]{2,1,0:T(8,128)(2,1)} %param.8) | copy-start | bytes 4718596
  6.5 73.7 %reduce-scatter.2.cloned.1.call-start = ((), (), s32[]{:S(2)}) async-start(), calls=%async_computation.1 | async-start | bytes 4718592 | tf_op jit(solution)/shard_map/reduce_scatter | solution.py:37
  8.8 2.4 copy-start.3
  16.7 0.7 copy-start.5
  16.8 121.0 %all-reduce.6.cloned.1.call-start = ((), (), s32[]{:S(2)}) async-start(), calls=%async_computation.3 | async-start | bytes 2097152 | tf_op jit(solution)/shard_map/psum | solution.py:55
  84.0 53.8 %copy-start = (f32[128,1024]{1,0:T(8,128)S(1)}, f32[128,1024]{1,0:T(8,128)}, u32[]{:S(2)}) copy-start(f32[128,1024]{1,0:T(8,128)} %reduce-scatter.2.cloned.1.call-done) | copy-start | bytes 1572868
  84.0 53.8 %copy-start.2 = (bf16[2,512,512]{2,1,0:T(8,128)(2,1)S(1)}, bf16[2,512,512]{2,1,0:T(8,128)(2,1)}, u32[]{:S(2)}) copy-start(bf16[2,512,512]{2,1,0:T(8,128)(2,1)} %param.13) | copy-start | bytes 3145732
  85.4 138.7 %all-reduce.8.cloned.1.call-start = ((), (), s32[]{:S(2)}) async-start(), calls=%async_computation.4 | async-start | bytes 2097152 | tf_op jit(solution)/shard_map/psum | solution.py:55
  137.8 226.3 %all-reduce.4.cloned.1.call-start = ((), (), s32[]{:S(2)}) async-start(), calls=%async_computation.2 | async-start | bytes 524288 | tf_op jit(solution)/shard_map/psum | solution.py:9
  224.2 140.0 %copy-start.4 = (bf16[512,1024]{1,0:T(8,128)(2,1)S(1)}, bf16[512,1024]{1,0:T(8,128)(2,1)}, u32[]{:S(2)}) copy-start(bf16[512,1024]{1,0:T(8,128)(2,1)} %all-reduce.8.cloned.1.call-done) | copy-start | bytes 3145732
Sparse Core Ops, SparseCore 0:
  16.9 63.3 reduce-scatter.1
  85.6 52.1 all-reduce.5
  140.3 83.8 all-reduce.7
  227.2 136.9 all-reduce.3
